TPU v7x, 32 devices: a whole 2x2x4 slice. The times are simulated.
32 devices in a mesh: gx: 8 (over y, x, core), gy: 4 (over z).
Axes of the slice: x: 2, y: 2, z: 4, core: 2. Of those that a mesh axis runs over, the one named last changes fastest.
Arguments:
- grad_p: float32 [3, 128, 64, 128], P(None, 'gx', 'gy'), may hold values from -6 to 6
- grad_s: float32 [3, 128, 64, 128], P(None, 'gx', 'gy'), may hold values from -6 to 6
- acc_p: float32 [128, 64, 128], P('gx', 'gy'), may hold values from 0.2 to 2
- acc_s: float32 [128, 64, 128], P('gx', 'gy'), may hold values from 0.2 to 2
- trans_x: float32 [128, 64, 128], P('gx', 'gy'), may hold values from 0.1 to 10
- trans_y: float32 [128, 64, 128], P('gx', 'gy'), may hold values from 0.1 to 10
- trans_z: float32 [128, 64, 128], P('gx', 'gy'), may hold values from 0.1 to 10
- c_pp: float32 [3, 128, 64, 128], P(None, 'gx', 'gy'), may hold values from 0.05 to 0.5
- c_ss: float32 [3, 128, 64, 128], P(None, 'gx', 'gy'), may hold values from 0.2 to 2
- c_ps: float32 [3, 128, 64, 128], P(None, 'gx', 'gy'), may hold values from -0.2 to 0.2
- c_sp: float32 [3, 128, 64, 128], P(None, 'gx', 'gy'), may hold values from -0.5 to 0.5
- frac: float32 [3, 128, 64, 128], P(None, 'gx', 'gy'), may hold values from 0 to 0.5
- mobility: float32 [3, 128, 64, 128], P(None, 'gx', 'gy'), may hold values from 0.5 to 2
- rate_mis: float32 [64, 3], P(('gx', 'gy')), may hold values from -6 to 6
- bhp_mis: float32 [64, 3], P(('gx', 'gy')), may hold values from -6 to 6
- control: int32 [64, 3], P(('gx', 'gy')), may hold values from 0 to 1
- perf_well: int32 [4096], P(('gx', 'gy')), may hold values from 0 to 63
- perf_cell: int32 [4096], P(('gx', 'gy')), may hold values from 0 to 32767
- perf_wi: float32 [4096], P(('gx', 'gy')), may hold values from 1 to 10
Outputs:
- lam_p: float32 [128, 64, 128], P('gx', 'gy')
- lam_s: float32 [128, 64, 128], P('gx', 'gy')
- well_grad: float32 [64, 3], P(('gx', 'gy'))
Inputs may be any that keep to these rules, and one draw needn't show every extreme that they name: perf_cell indexes the block of the device that holds the slot, as (i * 16 + j) * 128 + k; slots may share a cell. `perf_well`: well w is held by the device of flat index w // 2 along gx+gy; a well's slots may lie on any devices.
All inputs are finite; a program needn't handle non-finite values.
Results may differ from a plain program's by a relative error of at most 0.0002.
Values sent between devices are 32-bit elements; how exact they have to be, the bound alone decides.
No kernel may reach another device: no remote copies, remote signals or barrier semaphores. Data moves between devices by JAX's collectives and lax.ppermute only.
A program may use at most 128 MiB of HBM per device.

v0:
```python
import jax
import jax.numpy as jnp
from jax import lax
from jax.sharding import PartitionSpec as P

SWEEPS = 8
omega_factor = 0.8


def passed_along(value, axis, by):
    length = lax.axis_size(axis)
    pairs = [(i, i + by) for i in range(length) if 0 <= i + by < length]
    return lax.ppermute(value, axis, pairs)


def padded_2(block, sides, width):
    for axis, dim in sides:
        count = lax.axis_size(axis)
        forward = [(i, i + 1) for i in range(count - 1)]
        backward = [(target, source) for source, target in forward]
        low = lax.ppermute(
            lax.slice_in_dim(block, block.shape[dim] - width, None, axis=dim), axis, forward
        )
        high = lax.ppermute(lax.slice_in_dim(block, 0, width, axis=dim), axis, backward)
        block = jnp.concatenate([low, block, high], axis=dim)
    return block


def neighbour_sum(fields, table):
    centre = fields[:, 1:-1, 1:-1, :]
    east = fields[:, 2:, 1:-1, :]
    west = fields[:, :-2, 1:-1, :]
    north = fields[:, 1:-1, 2:, :]
    south = fields[:, 1:-1, :-2, :]
    upper = jnp.pad(centre[..., 1:], ((0, 0), (0, 0), (0, 0), (0, 1)))
    lower = jnp.pad(centre[..., :-1], ((0, 0), (0, 0), (0, 0), (1, 0)))
    total = table[8] * east + table[9] * west
    total = total + table[10] * north + table[11] * south
    total = total + table[12] * upper + table[13] * lower
    return (centre, total)


def relax(fields, table):
    centre, beside_all = neighbour_sum(fields, table)
    weight_sum = table[14]
    laplace = weight_sum * centre - beside_all
    old_a = centre[0]
    old_b = centre[1]
    out_a = table[0] * old_a + laplace[0] + table[3] * old_b + table[4] * laplace[1]
    out_b = table[2] * old_a + table[1] * old_b + table[5] * laplace[1]
    new_a = old_a + table[15] * (table[6] - out_a)
    new_b = old_b + table[16] * (table[7] - out_b)
    return jnp.stack([new_a, new_b])


def local(
    grad_p,
    grad_s,
    acc_p,
    acc_s,
    trans_x,
    trans_y,
    trans_z,
    c_pp,
    c_ss,
    c_ps,
    c_sp,
    frac,
    mobility,
    rate_mis,
    bhp_mis,
    control,
    perf_well,
    perf_cell,
    perf_wi,
):
    rows_x, rows_y, layers = trans_x.shape
    steps = grad_p.shape[0]
    sweeps = SWEEPS
    cells = rows_x * rows_y * layers
    gx_at = lax.axis_index("gx")
    gy_at = lax.axis_index("gy")
    east_plane = passed_along(trans_x[0:1], "gx", -1)
    north_plane = passed_along(trans_y[:, 0:1], "gy", -1)
    first_x = lax.broadcasted_iota(jnp.int32, (rows_x, 1, 1), 0) + gx_at * rows_x > 0
    first_y = lax.broadcasted_iota(jnp.int32, (1, rows_y, 1), 1) + gy_at * rows_y > 0
    first_z = lax.broadcasted_iota(jnp.int32, (1, 1, layers), 2) > 0
    w_east = jnp.concatenate([trans_x[1:], east_plane], axis=0)
    w_west = jnp.where(first_x, trans_x, 0.0)
    w_north = jnp.concatenate([trans_y[:, 1:], north_plane], axis=1)
    w_south = jnp.where(first_y, trans_y, 0.0)
    w_up = jnp.pad(trans_z[:, :, 1:], ((0, 0), (0, 0), (0, 1)))
    w_down = jnp.where(first_z, trans_z, 0.0)
    weight_sum = w_east + w_west + w_north + w_south + w_up + w_down
    effective = jnp.where(control == 1, rate_mis, bhp_mis)
    all_rows = lax.all_gather(effective, ("gx", "gy"), axis=0, tiled=True)
    well_count = all_rows.shape[0]
    selector = (perf_well[:, None] == jnp.arange(well_count, dtype=jnp.int32)[None, :]).astype(
        jnp.float32
    )
    perf_rows = jnp.dot(selector, all_rows, precision=lax.Precision.HIGHEST)
    sources = (
        jnp.zeros((steps, cells), jnp.float32)
        .at[:, perf_cell]
        .add((perf_wi[:, None] * perf_rows).T)
    )
    sources = sources.reshape(steps, rows_x, rows_y, layers)
    multipliers = jnp.zeros((2, rows_x, rows_y, layers), jnp.float32)
    returned = [None] * steps
    for step_index in reversed(range(steps)):
        right_a = grad_p[step_index] + sources[step_index] + acc_p * multipliers[0]
        right_b = grad_s[step_index] + acc_s * multipliers[1]
        scale_a = omega_factor / (c_pp[step_index] + weight_sum)
        scale_b = omega_factor / (c_ss[step_index] + mobility[step_index] * weight_sum)
        table = jnp.stack(
            [
                c_pp[step_index],
                c_ss[step_index],
                c_ps[step_index],
                c_sp[step_index],
                frac[step_index],
                mobility[step_index],
                right_a,
                right_b,
                w_east,
                w_west,
                w_north,
                w_south,
                w_up,
                w_down,
                weight_sum,
                scale_a,
                scale_b,
            ]
        )
        for sweep_index in range(sweeps):
            padded = padded_2(multipliers, (("gx", 1), ("gy", 2)), 1)
            multipliers = relax(padded, table)
        flat_fields = multipliers.reshape(2, cells)
        at_cells = flat_fields[:, perf_cell]
        at_frac = frac[step_index].reshape(cells)[perf_cell]
        returned[step_index] = perf_wi * (at_cells[0] + at_frac * at_cells[1])
    contributions = jnp.stack(returned, axis=1)
    dense = jnp.dot(selector.T, contributions, precision=lax.Precision.HIGHEST)
    well_grad = lax.psum_scatter(dense, ("gx", "gy"), scatter_dimension=0, tiled=True)
    return (multipliers[0], multipliers[1], well_grad)


def solution(mesh):
    placed = (
        P(None, "gx", "gy", None),
        P(None, "gx", "gy", None),
        P("gx", "gy", None),
        P("gx", "gy", None),
        P("gx", "gy", None),
        P("gx", "gy", None),
        P("gx", "gy", None),
        P(None, "gx", "gy", None),
        P(None, "gx", "gy", None),
        P(None, "gx", "gy", None),
        P(None, "gx", "gy", None),
        P(None, "gx", "gy", None),
        P(None, "gx", "gy", None),
        P(("gx", "gy"), None),
        P(("gx", "gy"), None),
        P(("gx", "gy"), None),
        P(("gx", "gy")),
        P(("gx", "gy")),
        P(("gx", "gy")),
    )
    return jax.shard_map(
        local,
        mesh=mesh,
        in_specs=placed,
        out_specs=(P("gx", "gy", None), P("gx", "gy", None), P(("gx", "gy"), None)),
        check_vma=False,
    )
```

profile of v0, /device:TPU:0, one launch (start us, length us, event | category | flops | bytes accessed | tf_op | source)
XLA Modules:
  0.0 621.0 jit_solution(6534651151224634101)
XLA Ops:
  10.5 71.9 %all-gather = f32[32,2,3]{2,1,0:T(2,128)S(1)} all-gather(f32[1,2,3]{2,1,0:T(2,128)S(1)} %fusion.643), channel_id=1, replica_groups=mesh['gx'=8,'gy'=4] {'gx','gy'}, dimensions={0}, use_global_device_ids=true | all-gather | bytes 792 | tf_op jit(solution)/shard_map/all_gather | solution.py:96
  83.4 7.8 %scatter_custom_fusion = f32[3,32768]{0,1:T(8,128)} fusion(s32[128]{0:T(128)S(1)} %compare_select_fusion, f32[128,3]{1,0:T(8,128)S(1)} %copy.30, f32[]{:T(128)} %constant.14.clone.1), kind=kCustom, calls=%fused_computation.10 | custom fusion | flops 384 | bytes 393220 | tf_op jit(solution)/shard_map/scatter-add | solution.py:105
  91.4 30.5 %slice_reduce_fusion = (f32[32768]{0:T(1024)S(1)}, f32[32768]{0:T(1024)S(1)}, f32[32768]{0:T(1024)S(1)}) fusion(f32[3,32768]{0,1:T(8,128)} %scatter_custom_fusion), kind=kLoop, calls=%fused_computation.7 | loop fusion | bytes 786432 | tf_op jit(solution)/shard_map/slice | solution.py:111
  136.6 4.8 collective-permute-start.9
  149.7 4.8 collective-permute-start.13
  173.6 5.1 collective-permute-start.19
  180.9 4.7 collective-permute-start.21
  189.8 5.1 collective-permute-start.23
  205.9 5.1 collective-permute-start.27
  222.1 5.1 collective-permute-start.31
  238.3 6.0 collective-permute-start.35
  254.3 6.0 collective-permute-start.39
  270.2 6.0 collective-permute-start.43
  287.3 6.0 collective-permute-start.47
  304.3 6.0 collective-permute-start.51
  321.4 6.0 collective-permute-start.55
  338.5 6.0 collective-permute-start.59
  355.6 6.0 collective-permute-start.63
  372.7 6.0 collective-permute-start.67
  388.7 6.0 collective-permute-start.71
  404.6 6.0 collective-permute-start.75
  421.7 6.6 %collective-permute-start.79 = (f32[2,1,16,128]{3,2,1,0:T(8,128)}, f32[2,1,16,128]{3,2,1,0:T(8,128)}, u32[]{:S(2)}, u32[]{:S(2)}) collective-permute-start(f32[2,1,16,128]{3,2,1,0:T(8,128)} %get-tuple-element.147), channel_id=1, source_target_pairs={{0,4},{4,8},{8,12},{12,16},{16,20},{20,24},{24,28},{1,5},{5,9},{9,... | collective-permute-start | bytes 49160 | tf_op jit(solution)/shard_map/ppermute | solution.py:21
  450.2 6.6 %collective-permute-start.83 = (f32[2,1,16,128]{3,2,1,0:T(8,128)}, f32[2,1,16,128]{3,2,1,0:T(8,128)}, u32[]{:S(2)}, u32[]{:S(2)}) collective-permute-start(f32[2,1,16,128]{3,2,1,0:T(8,128)} %get-tuple-element.143), channel_id=1, source_target_pairs={{0,4},{4,8},{8,12},{12,16},{16,20},{20,24},{24,28},{1,5},{5,9},{9,... | collective-permute-start | bytes 49160 | tf_op jit(solution)/shard_map/ppermute | solution.py:21
  458.7 8.9 %copy.33 = f32[2,32768]{0,1:T(8,128)} copy(f32[2,32768]{1,0:T(2,128)} %pad_maximum_fusion.307) | data formatting | bytes 524288 | tf_op jit(solution)/shard_map/stack | solution.py:53
  467.6 7.1 %gather_fusion.4 = f32[128,2]{1,0:T(8,128)} fusion(f32[2,32768]{0,1:T(8,128)} %copy.33, s32[1024]{0:T(1024)} %pad_clamp_fusion), kind=kCustom, calls=%fused_computation.4 | custom fusion | bytes 2560 | tf_op jit(solution)/shard_map/gather | solution.py:140
  487.3 5.5 collective-permute-start.87
  505.7 6.6 %collective-permute-start.91 = (f32[2,1,16,128]{3,2,1,0:T(8,128)}, f32[2,1,16,128]{3,2,1,0:T(8,128)}, u32[]{:S(2)}, u32[]{:S(2)}) collective-permute-start(f32[2,1,16,128]{3,2,1,0:T(8,128)} %get-tuple-element.135), channel_id=1, source_target_pairs={{0,4},{4,8},{8,12},{12,16},{16,20},{20,24},{24,28},{1,5},{5,9},{9,... | collective-permute-start | bytes 49160 | tf_op jit(solution)/shard_map/ppermute | solution.py:21
  514.2 8.9 %copy.32 = f32[2,32768]{0,1:T(8,128)} copy(f32[2,32768]{1,0:T(2,128)} %pad_maximum_fusion.306) | data formatting | bytes 524288 | tf_op jit(solution)/shard_map/stack | solution.py:53
  523.1 7.1 %gather_fusion.2 = f32[128,2]{1,0:T(8,128)} fusion(f32[2,32768]{0,1:T(8,128)} %copy.32, s32[1024]{0:T(1024)} %pad_clamp_fusion), kind=kCustom, calls=%fused_computation.2 | custom fusion | bytes 2560 | tf_op jit(solution)/shard_map/gather | solution.py:140
  557.4 8.4 %copy.31 = f32[2,32768]{0,1:T(8,128)} copy(f32[2,32768]{1,0:T(2,128)S(1)} %pad_maximum_fusion.305) | data formatting | bytes 524288 | tf_op jit(solution)/shard_map/stack | solution.py:53
  565.8 6.5 %gather_fusion = f32[128,2]{1,0:T(8,128)S(1)} fusion(f32[2,32768]{0,1:T(8,128)} %copy.31, s32[1024]{0:T(1024)} %pad_clamp_fusion), kind=kCustom, calls=%fused_computation | custom fusion | bytes 2560 | tf_op jit(solution)/shard_map/gather | solution.py:140
  572.9 47.6 %all-reduce.51 = f32[64,3]{1,0:T(8,128)S(1)} all-reduce(f32[64,3]{1,0:T(8,128)S(1)} %fusion.588), channel_id=2, replica_groups=mesh['gx'=8,'gy'=4] {'gx','gy'}, use_global_device_ids=true, to_apply=%region_1.2.clone | all-reduce | flops 192 | bytes 1536
  (398 shorter events, 286.7 us)
Async XLA Ops:
  0.6 121.5 %collective-permute-start.2 = (f32[2,1,16,128]{3,2,1,0:T(8,128)S(1)}, f32[2,1,16,128]{3,2,1,0:T(8,128)S(1)}, u32[]{:S(2)}, u32[]{:S(2)}) collective-permute-start(f32[2,1,16,128]{3,2,1,0:T(8,128)S(1)} %broadcast.163), channel_id=1, source_target_pairs={{4,0},{8,4},{12,8},{16,12},{20,16},{24,20},{28,24},{5,1},{9,5},{13... | collective-permute-start | bytes 49160 | tf_op jit(solution)/shard_map/ppermute | solution.py:24
  1.9 120.2 %collective-permute-start.3 = (f32[2,1,16,128]{3,2,1,0:T(8,128)S(1)}, f32[2,1,16,128]{3,2,1,0:T(8,128)S(1)}, u32[]{:S(2)}, u32[]{:S(2)}) collective-permute-start(f32[2,1,16,128]{3,2,1,0:T(8,128)S(1)} %broadcast.163), channel_id=1, source_target_pairs={{0,4},{4,8},{8,12},{12,16},{16,20},{20,24},{24,28},{1,5},{5,9},{9,... | collective-permute-start | bytes 49160 | tf_op jit(solution)/shard_map/ppermute | solution.py:21
  5.7 116.3 %collective-permute-start = (f32[1,16,128]{2,1,0:T(8,128)S(1)}, f32[1,16,128]{2,1,0:T(8,128)S(1)}, u32[]{:S(2)}, u32[]{:S(2)}) collective-permute-start(f32[1,16,128]{2,1,0:T(8,128)S(1)} %slice.1103), channel_id=1, source_target_pairs={{4,0},{8,4},{12,8},{16,12},{20,16},{24,20},{28,24},{5,1},{9,5},{13... | collective-permute-start | bytes 24584 | tf_op jit(solution)/shard_map/ppermute | solution.py:13
  7.8 114.2 %collective-permute-start.1 = (f32[16,1,128]{2,1,0:T(1,128)S(1)}, f32[16,1,128]{2,1,0:T(1,128)S(1)}, u32[]{:S(2)}, u32[]{:S(2)}) collective-permute-start(f32[16,1,128]{2,1,0:T(1,128)S(1)} %slice.1105), channel_id=1, source_target_pairs={{1,0},{2,1},{3,2},{5,4},{6,5},{7,6},{9,8},{10,9},{11,10},{13,12},{... | collective-permute-start | bytes 24584 | tf_op jit(solution)/shard_map/ppermute | solution.py:13
  237.0 7.4 %collective-permute-start.34 = (f32[2,1,16,128]{3,2,1,0:T(8,128)S(1)}, f32[2,1,16,128]{3,2,1,0:T(8,128)S(1)}, u32[]{:S(2)}, u32[]{:S(2)}) collective-permute-start(f32[2,1,16,128]{3,2,1,0:T(8,128)S(1)} %get-tuple-element.192), channel_id=1, source_target_pairs={{4,0},{8,4},{12,8},{16,12},{20,16},{24,20},{28,24},{5,1},{9,5},{13... | collective-permute-start | bytes 49160 | tf_op jit(solution)/shard_map/ppermute | solution.py:24
  238.3 6.9 %collective-permute-start.35 = (f32[2,1,16,128]{3,2,1,0:T(8,128)S(1)}, f32[2,1,16,128]{3,2,1,0:T(8,128)S(1)}, u32[]{:S(2)}, u32[]{:S(2)}) collective-permute-start(f32[2,1,16,128]{3,2,1,0:T(8,128)S(1)} %get-tuple-element.191), channel_id=1, source_target_pairs={{0,4},{4,8},{8,12},{12,16},{16,20},{20,24},{24,28},{1,5},{5,9},{9,... | collective-permute-start | bytes 49160 | tf_op jit(solution)/shard_map/ppermute | solution.py:21
  253.0 7.4 %collective-permute-start.38 = (f32[2,1,16,128]{3,2,1,0:T(8,128)S(1)}, f32[2,1,16,128]{3,2,1,0:T(8,128)S(1)}, u32[]{:S(2)}, u32[]{:S(2)}) collective-permute-start(f32[2,1,16,128]{3,2,1,0:T(8,128)S(1)} %get-tuple-element.188), channel_id=1, source_target_pairs={{4,0},{8,4},{12,8},{16,12},{20,16},{24,20},{28,24},{5,1},{9,5},{13... | collective-permute-start | bytes 49160 | tf_op jit(solution)/shard_map/ppermute | solution.py:24
  254.3 6.9 %collective-permute-start.39 = (f32[2,1,16,128]{3,2,1,0:T(8,128)S(1)}, f32[2,1,16,128]{3,2,1,0:T(8,128)S(1)}, u32[]{:S(2)}, u32[]{:S(2)}) collective-permute-start(f32[2,1,16,128]{3,2,1,0:T(8,128)S(1)} %get-tuple-element.187), channel_id=1, source_target_pairs={{0,4},{4,8},{8,12},{12,16},{16,20},{20,24},{24,28},{1,5},{5,9},{9,... | collective-permute-start | bytes 49160 | tf_op jit(solution)/shard_map/ppermute | solution.py:21
  268.9 7.4 %collective-permute-start.42 = (f32[2,1,16,128]{3,2,1,0:T(8,128)S(1)}, f32[2,1,16,128]{3,2,1,0:T(8,128)S(1)}, u32[]{:S(2)}, u32[]{:S(2)}) collective-permute-start(f32[2,1,16,128]{3,2,1,0:T(8,128)S(1)} %get-tuple-element.184), channel_id=1, source_target_pairs={{4,0},{8,4},{12,8},{16,12},{20,16},{24,20},{28,24},{5,1},{9,5},{13... | collective-permute-start | bytes 49160 | tf_op jit(solution)/shard_map/ppermute | solution.py:24
  270.2 6.9 %collective-permute-start.43 = (f32[2,1,16,128]{3,2,1,0:T(8,128)S(1)}, f32[2,1,16,128]{3,2,1,0:T(8,128)S(1)}, u32[]{:S(2)}, u32[]{:S(2)}) collective-permute-start(f32[2,1,16,128]{3,2,1,0:T(8,128)S(1)} %get-tuple-element.183), channel_id=1, source_target_pairs={{0,4},{4,8},{8,12},{12,16},{16,20},{20,24},{24,28},{1,5},{5,9},{9,... | collective-permute-start | bytes 49160 | tf_op jit(solution)/shard_map/ppermute | solution.py:21
  286.0 7.4 %collective-permute-start.46 = (f32[2,1,16,128]{3,2,1,0:T(8,128)S(1)}, f32[2,1,16,128]{3,2,1,0:T(8,128)S(1)}, u32[]{:S(2)}, u32[]{:S(2)}) collective-permute-start(f32[2,1,16,128]{3,2,1,0:T(8,128)S(1)} %get-tuple-element.180), channel_id=1, source_target_pairs={{4,0},{8,4},{12,8},{16,12},{20,16},{24,20},{28,24},{5,1},{9,5},{13... | collective-permute-start | bytes 49160 | tf_op jit(solution)/shard_map/ppermute | solution.py:24
  287.3 6.9 %collective-permute-start.47 = (f32[2,1,16,128]{3,2,1,0:T(8,128)S(1)}, f32[2,1,16,128]{3,2,1,0:T(8,128)S(1)}, u32[]{:S(2)}, u32[]{:S(2)}) collective-permute-start(f32[2,1,16,128]{3,2,1,0:T(8,128)S(1)} %get-tuple-element.179), channel_id=1, source_target_pairs={{0,4},{4,8},{8,12},{12,16},{16,20},{20,24},{24,28},{1,5},{5,9},{9,... | collective-permute-start | bytes 49160 | tf_op jit(solution)/shard_map/ppermute | solution.py:21
  303.0 7.4 %collective-permute-start.50 = (f32[2,1,16,128]{3,2,1,0:T(8,128)S(1)}, f32[2,1,16,128]{3,2,1,0:T(8,128)S(1)}, u32[]{:S(2)}, u32[]{:S(2)}) collective-permute-start(f32[2,1,16,128]{3,2,1,0:T(8,128)S(1)} %get-tuple-element.176), channel_id=1, source_target_pairs={{4,0},{8,4},{12,8},{16,12},{20,16},{24,20},{28,24},{5,1},{9,5},{13... | collective-permute-start | bytes 49160 | tf_op jit(solution)/shard_map/ppermute | solution.py:24
  304.3 6.9 %collective-permute-start.51 = (f32[2,1,16,128]{3,2,1,0:T(8,128)S(1)}, f32[2,1,16,128]{3,2,1,0:T(8,128)S(1)}, u32[]{:S(2)}, u32[]{:S(2)}) collective-permute-start(f32[2,1,16,128]{3,2,1,0:T(8,128)S(1)} %get-tuple-element.175), channel_id=1, source_target_pairs={{0,4},{4,8},{8,12},{12,16},{16,20},{20,24},{24,28},{1,5},{5,9},{9,... | collective-permute-start | bytes 49160 | tf_op jit(solution)/shard_map/ppermute | solution.py:21
  320.1 7.4 %collective-permute-start.54 = (f32[2,1,16,128]{3,2,1,0:T(8,128)S(1)}, f32[2,1,16,128]{3,2,1,0:T(8,128)S(1)}, u32[]{:S(2)}, u32[]{:S(2)}) collective-permute-start(f32[2,1,16,128]{3,2,1,0:T(8,128)S(1)} %get-tuple-element.172), channel_id=1, source_target_pairs={{4,0},{8,4},{12,8},{16,12},{20,16},{24,20},{28,24},{5,1},{9,5},{13... | collective-permute-start | bytes 49160 | tf_op jit(solution)/shard_map/ppermute | solution.py:24
  337.2 7.4 %collective-permute-start.58 = (f32[2,1,16,128]{3,2,1,0:T(8,128)S(1)}, f32[2,1,16,128]{3,2,1,0:T(8,128)S(1)}, u32[]{:S(2)}, u32[]{:S(2)}) collective-permute-start(f32[2,1,16,128]{3,2,1,0:T(8,128)S(1)} %get-tuple-element.168), channel_id=1, source_target_pairs={{4,0},{8,4},{12,8},{16,12},{20,16},{24,20},{28,24},{5,1},{9,5},{13... | collective-permute-start | bytes 49160 | tf_op jit(solution)/shard_map/ppermute | solution.py:24
  354.3 7.4 %collective-permute-start.62 = (f32[2,1,16,128]{3,2,1,0:T(8,128)S(1)}, f32[2,1,16,128]{3,2,1,0:T(8,128)S(1)}, u32[]{:S(2)}, u32[]{:S(2)}) collective-permute-start(f32[2,1,16,128]{3,2,1,0:T(8,128)S(1)} %get-tuple-element.164), channel_id=1, source_target_pairs={{4,0},{8,4},{12,8},{16,12},{20,16},{24,20},{28,24},{5,1},{9,5},{13... | collective-permute-start | bytes 49160 | tf_op jit(solution)/shard_map/ppermute | solution.py:24
  371.4 7.4 %collective-permute-start.66 = (f32[2,1,16,128]{3,2,1,0:T(8,128)S(1)}, f32[2,1,16,128]{3,2,1,0:T(8,128)S(1)}, u32[]{:S(2)}, u32[]{:S(2)}) collective-permute-start(f32[2,1,16,128]{3,2,1,0:T(8,128)S(1)} %get-tuple-element.160), channel_id=1, source_target_pairs={{4,0},{8,4},{12,8},{16,12},{20,16},{24,20},{28,24},{5,1},{9,5},{13... | collective-permute-start | bytes 49160 | tf_op jit(solution)/shard_map/ppermute | solution.py:24
  387.4 7.4 %collective-permute-start.70 = (f32[2,1,16,128]{3,2,1,0:T(8,128)S(1)}, f32[2,1,16,128]{3,2,1,0:T(8,128)S(1)}, u32[]{:S(2)}, u32[]{:S(2)}) collective-permute-start(f32[2,1,16,128]{3,2,1,0:T(8,128)S(1)} %get-tuple-element.156), channel_id=1, source_target_pairs={{4,0},{8,4},{12,8},{16,12},{20,16},{24,20},{28,24},{5,1},{9,5},{13... | collective-permute-start | bytes 49160 | tf_op jit(solution)/shard_map/ppermute | solution.py:24
  403.3 8.1 %collective-permute-start.74 = (f32[2,1,16,128]{3,2,1,0:T(8,128)S(1)}, f32[2,1,16,128]{3,2,1,0:T(8,128)S(1)}, u32[]{:S(2)}, u32[]{:S(2)}) collective-permute-start(f32[2,1,16,128]{3,2,1,0:T(8,128)S(1)} %get-tuple-element.152), channel_id=1, source_target_pairs={{4,0},{8,4},{12,8},{16,12},{20,16},{24,20},{28,24},{5,1},{9,5},{13... | collective-permute-start | bytes 49160 | tf_op jit(solution)/shard_map/ppermute | solution.py:24
  420.4 16.0 %collective-permute-start.78 = (f32[2,1,16,128]{3,2,1,0:T(8,128)}, f32[2,1,16,128]{3,2,1,0:T(8,128)S(1)}, u32[]{:S(2)}, u32[]{:S(2)}) collective-permute-start(f32[2,1,16,128]{3,2,1,0:T(8,128)} %get-tuple-element.148), channel_id=1, source_target_pairs={{4,0},{8,4},{12,8},{16,12},{20,16},{24,20},{28,24},{5,1},{9,5},{13... | collective-permute-start | bytes 49160 | tf_op jit(solution)/shard_map/ppermute | solution.py:24
  421.7 14.7 %collective-permute-start.79 = (f32[2,1,16,128]{3,2,1,0:T(8,128)}, f32[2,1,16,128]{3,2,1,0:T(8,128)}, u32[]{:S(2)}, u32[]{:S(2)}) collective-permute-start(f32[2,1,16,128]{3,2,1,0:T(8,128)} %get-tuple-element.147), channel_id=1, source_target_pairs={{0,4},{4,8},{8,12},{12,16},{16,20},{20,24},{24,28},{1,5},{5,9},{9,... | collective-permute-start | bytes 49160 | tf_op jit(solution)/shard_map/ppermute | solution.py:21
  437.4 7.1 %collective-permute-start.80 = (f32[2,18,1,128]{3,2,1,0:T(1,128)S(1)}, f32[2,18,1,128]{3,2,1,0:T(1,128)S(1)}, u32[]{:S(2)}, u32[]{:S(2)}) collective-permute-start(f32[2,18,1,128]{3,2,1,0:T(1,128)S(1)} %get-tuple-element.89), channel_id=1, source_target_pairs={{1,0},{2,1},{3,2},{5,4},{6,5},{7,6},{9,8},{10,9},{11,10},{13,12},{... | collective-permute-start | bytes 55304 | tf_op jit(solution)/shard_map/ppermute | solution.py:24
  448.9 25.9 %collective-permute-start.82 = (f32[2,1,16,128]{3,2,1,0:T(8,128)}, f32[2,1,16,128]{3,2,1,0:T(8,128)S(1)}, u32[]{:S(2)}, u32[]{:S(2)}) collective-permute-start(f32[2,1,16,128]{3,2,1,0:T(8,128)} %get-tuple-element.144), channel_id=1, source_target_pairs={{4,0},{8,4},{12,8},{16,12},{20,16},{24,20},{28,24},{5,1},{9,5},{13... | collective-permute-start | bytes 49160 | tf_op jit(solution)/shard_map/ppermute | solution.py:24
  450.2 24.6 %collective-permute-start.83 = (f32[2,1,16,128]{3,2,1,0:T(8,128)}, f32[2,1,16,128]{3,2,1,0:T(8,128)}, u32[]{:S(2)}, u32[]{:S(2)}) collective-permute-start(f32[2,1,16,128]{3,2,1,0:T(8,128)} %get-tuple-element.143), channel_id=1, source_target_pairs={{0,4},{4,8},{8,12},{12,16},{16,20},{20,24},{24,28},{1,5},{5,9},{9,... | collective-permute-start | bytes 49160 | tf_op jit(solution)/shard_map/ppermute | solution.py:21
  475.7 7.1 %collective-permute-start.84 = (f32[2,18,1,128]{3,2,1,0:T(1,128)S(1)}, f32[2,18,1,128]{3,2,1,0:T(1,128)S(1)}, u32[]{:S(2)}, u32[]{:S(2)}) collective-permute-start(f32[2,18,1,128]{3,2,1,0:T(1,128)S(1)} %get-tuple-element.87), channel_id=1, source_target_pairs={{1,0},{2,1},{3,2},{5,4},{6,5},{7,6},{9,8},{10,9},{11,10},{13,12},{... | collective-permute-start | bytes 55304 | tf_op jit(solution)/shard_map/ppermute | solution.py:24
  486.0 8.4 %collective-permute-start.86 = (f32[2,1,16,128]{3,2,1,0:T(8,128)S(1)}, f32[2,1,16,128]{3,2,1,0:T(8,128)S(1)}, u32[]{:S(2)}, u32[]{:S(2)}) collective-permute-start(f32[2,1,16,128]{3,2,1,0:T(8,128)S(1)} %get-tuple-element.140), channel_id=1, source_target_pairs={{4,0},{8,4},{12,8},{16,12},{20,16},{24,20},{28,24},{5,1},{9,5},{13... | collective-permute-start | bytes 49160 | tf_op jit(solution)/shard_map/ppermute | solution.py:24
  487.3 7.2 %collective-permute-start.87 = (f32[2,1,16,128]{3,2,1,0:T(8,128)S(1)}, f32[2,1,16,128]{3,2,1,0:T(8,128)S(1)}, u32[]{:S(2)}, u32[]{:S(2)}) collective-permute-start(f32[2,1,16,128]{3,2,1,0:T(8,128)S(1)} %get-tuple-element.139), channel_id=1, source_target_pairs={{0,4},{4,8},{8,12},{12,16},{16,20},{20,24},{24,28},{1,5},{5,9},{9,... | collective-permute-start | bytes 49160 | tf_op jit(solution)/shard_map/ppermute | solution.py:21
  504.4 25.8 %collective-permute-start.90 = (f32[2,1,16,128]{3,2,1,0:T(8,128)}, f32[2,1,16,128]{3,2,1,0:T(8,128)S(1)}, u32[]{:S(2)}, u32[]{:S(2)}) collective-permute-start(f32[2,1,16,128]{3,2,1,0:T(8,128)} %get-tuple-element.136), channel_id=1, source_target_pairs={{4,0},{8,4},{12,8},{16,12},{20,16},{24,20},{28,24},{5,1},{9,5},{13... | collective-permute-start | bytes 49160 | tf_op jit(solution)/shard_map/ppermute | solution.py:24
  505.7 24.6 %collective-permute-start.91 = (f32[2,1,16,128]{3,2,1,0:T(8,128)}, f32[2,1,16,128]{3,2,1,0:T(8,128)}, u32[]{:S(2)}, u32[]{:S(2)}) collective-permute-start(f32[2,1,16,128]{3,2,1,0:T(8,128)} %get-tuple-element.135), channel_id=1, source_target_pairs={{0,4},{4,8},{8,12},{12,16},{16,20},{20,24},{24,28},{1,5},{5,9},{9,... | collective-permute-start | bytes 49160 | tf_op jit(solution)/shard_map/ppermute | solution.py:21
  531.2 7.1 %collective-permute-start.92 = (f32[2,18,1,128]{3,2,1,0:T(1,128)S(1)}, f32[2,18,1,128]{3,2,1,0:T(1,128)S(1)}, u32[]{:S(2)}, u32[]{:S(2)}) collective-permute-start(f32[2,18,1,128]{3,2,1,0:T(1,128)S(1)} %get-tuple-element.83), channel_id=1, source_target_pairs={{1,0},{2,1},{3,2},{5,4},{6,5},{7,6},{9,8},{10,9},{11,10},{13,12},{... | collective-permute-start | bytes 55304 | tf_op jit(solution)/shard_map/ppermute | solution.py:24
  541.5 6.9 %collective-permute-start.94 = (f32[2,1,16,128]{3,2,1,0:T(8,128)S(1)}, f32[2,1,16,128]{3,2,1,0:T(8,128)S(1)}, u32[]{:S(2)}, u32[]{:S(2)}) collective-permute-start(f32[2,1,16,128]{3,2,1,0:T(8,128)S(1)} %get-tuple-element.132), channel_id=1, source_target_pairs={{4,0},{8,4},{12,8},{16,12},{20,16},{24,20},{28,24},{5,1},{9,5},{13... | collective-permute-start | bytes 49160 | tf_op jit(solution)/shard_map/ppermute | solution.py:24
  (103 other events, 1747.1 us)
where the time goes:
time: 625 us; the launch traced here: 621 us
  starting transfers between devices  304 us (49%)
  blocking collectives  119 us (19%)
  local copies, waits for them, and re-layouts  93.1 us (15%)
  other arithmetic  58.7 us (9%)
  waiting for transfers between devices  41.7 us (7%)
    ppermute x48, starting transfers between devices, padded_2(): lax.ppermute(lax.slice_in_dim(block, block.shape[dim] - width, None, axis...  240 us
    all_gather x1, blocking collectives, local(): all_rows = lax.all_gather(effective, ('gx', 'gy'), axis=0, tiled=True)  71.9 us
    ppermute x48, starting transfers between devices, padded_2(): lax.ppermute(lax.slice_in_dim(block, 0, width, axis=dim), axis, backward)  62 us
    unnamed x1, blocking collectives  47.6 us
    ppermute x48, waiting for transfers between devices, padded_2(): lax.ppermute(lax.slice_in_dim(block, block.shape[dim] - width, None, axis...  41.6 us
    slice x1, local copies, waits for them, and re-layouts, local(): right_a = grad_p[step_index] + sources[step_index] + acc_p * multipliers[0]  30.5 us
    another operation x3, local copies, waits for them, and re-layouts, relax(): return jnp.stack([new_a, new_b])  26.2 us
    add x23, other arithmetic, relax(): new_b = old_b + table[16] * (table[7] - out_b)  22.6 us
  transfers between devices with their start and end apart: 98, of which 42 were waited for; matrix products, arithmetic and copies ran while one was open for 15% of the time, Pallas kernels for 0%

commit v1 on v0

--- a/solution.py
+++ b/solution.py
@@ -93,7 +93,19 @@
     w_down = jnp.where(first_z, trans_z, 0.0)
     weight_sum = w_east + w_west + w_north + w_south + w_up + w_down
     effective = jnp.where(control == 1, rate_mis, bhp_mis)
-    all_rows = lax.all_gather(effective, ("gx", "gy"), axis=0, tiled=True)
+    ways, here, step = (
+        lax.axis_size(("gx", "gy")),
+        lax.axis_index(("gx", "gy")),
+        effective.shape[0],
+    )
+    line, have = (effective, 1)
+    while have < ways:
+        line = jnp.concatenate(
+            [line, lax.ppermute(line, ("gx", "gy"), [(d, (d - have) % ways) for d in range(ways)])],
+            axis=0,
+        )
+        have = 2 * have
+    all_rows = jnp.roll(line, here * step, axis=0)
     well_count = all_rows.shape[0]
     selector = (perf_well[:, None] == jnp.arange(well_count, dtype=jnp.int32)[None, :]).astype(
         jnp.float32

time: 625 us -> 583 us (0.933)
  blocking collectives: 119 us -> 45.2 us
  starting transfers between devices: 304 us -> 317 us
  waiting for transfers between devices: 41.7 us -> 52.4 us
    all_gather x1 -> x0, blocking collectives: 71.9 us -> none  [local(): all_rows = lax.all_gather(effective, ('gx', 'gy'), axis=0, tiled=True)]
    ppermute x0 -> x5, starting transfers between devices: none -> 13.3 us  [local(): lax.ppermute(line, ('gx', 'gy'), [(d, (d - have) % ways) for d in range(w...]
  transfers between devices with their start and end apart: 98 -> 103, of which waited for: 42 -> 48; matrix products, arithmetic and copies ran while one was open for 15% -> 18% of each run, Pallas kernels for 0% -> 0%
where the time goes in v1:
time: 583 us; the launch traced here: 579 us
  starting transfers between devices  317 us (54%)
  local copies, waits for them, and re-layouts  98.3 us (17%)
  other arithmetic  61.7 us (11%)
  waiting for transfers between devices  52.4 us (9%)
  blocking collectives  45.2 us (8%)
    ppermute x48, starting transfers between devices, padded_2(): lax.ppermute(lax.slice_in_dim(block, block.shape[dim] - width, None, axis...  239 us
    ppermute x48, starting transfers between devices, padded_2(): lax.ppermute(lax.slice_in_dim(block, 0, width, axis=dim), axis, backward)  62.2 us
    unnamed x1, blocking collectives  45.2 us
    ppermute x48, waiting for transfers between devices, padded_2(): lax.ppermute(lax.slice_in_dim(block, block.shape[dim] - width, None, axis...  40.3 us
    slice x1, local copies, waits for them, and re-layouts, local(): right_a = grad_p[step_index] + sources[step_index] + acc_p * multipliers[0]  30.4 us
    another operation x3, local copies, waits for them, and re-layouts, relax(): return jnp.stack([new_a, new_b])  26 us
    add x23, other arithmetic, relax(): new_b = old_b + table[16] * (table[7] - out_b)  22.7 us
    gather x3, local copies, waits for them, and re-layouts, local(): at_cells = flat_fields[:, perf_cell]  20.8 us
  transfers between devices with their start and end apart: 103, of which 48 were waited for; matrix products, arithmetic and copies ran while one was open for 18% of the time, Pallas kernels for 0%

profile of v1, /device:TPU:0, one launch (start us, length us, event | category | flops | bytes accessed | tf_op | source)
XLA Modules:
  0.0 578.8 jit_solution(2827435444961159838)
XLA Ops:
  8.5 5.3 collective-permute-start.2
  36.9 7.8 %scatter_custom_fusion = f32[3,32768]{0,1:T(8,128)} fusion(s32[128]{0:T(128)S(1)} %compare_select_fusion, f32[128,3]{1,0:T(8,128)S(1)} %copy.33, f32[]{:T(128)} %constant.22.clone.1), kind=kCustom, calls=%fused_computation.10 | custom fusion | flops 384 | bytes 393220 | tf_op jit(solution)/shard_map/scatter-add | solution.py:117
  44.9 30.4 %slice_reduce_fusion = (f32[32768]{0:T(1024)S(1)}, f32[32768]{0:T(1024)S(1)}, f32[32768]{0:T(1024)S(1)}) fusion(f32[3,32768]{0,1:T(8,128)} %scatter_custom_fusion), kind=kLoop, calls=%fused_computation.7 | loop fusion | bytes 786432 | tf_op jit(solution)/shard_map/slice | solution.py:123
  108.4 5.0 collective-permute-start.18
  124.4 4.7 collective-permute-start.22
  133.3 5.1 collective-permute-start.24
  149.5 5.1 collective-permute-start.28
  165.7 5.1 collective-permute-start.32
  181.8 5.1 collective-permute-start.36
  198.0 5.1 collective-permute-start.40
  213.1 5.9 %collective-permute-start.44 = (f32[2,1,16,128]{3,2,1,0:T(8,128)S(1)}, f32[2,1,16,128]{3,2,1,0:T(8,128)S(1)}, u32[]{:S(2)}, u32[]{:S(2)}) collective-permute-start(f32[2,1,16,128]{3,2,1,0:T(8,128)S(1)} %get-tuple-element.187), channel_id=1, source_target_pairs={{0,4},{4,8},{8,12},{12,16},{16,20},{20,24},{24,28},{1,5},{5,9},{9,... | collective-permute-start | bytes 49160 | tf_op jit(solution)/shard_map/ppermute | solution.py:21
  228.8 6.0 %collective-permute-start.48 = (f32[2,1,16,128]{3,2,1,0:T(8,128)S(1)}, f32[2,1,16,128]{3,2,1,0:T(8,128)S(1)}, u32[]{:S(2)}, u32[]{:S(2)}) collective-permute-start(f32[2,1,16,128]{3,2,1,0:T(8,128)S(1)} %get-tuple-element.183), channel_id=1, source_target_pairs={{0,4},{4,8},{8,12},{12,16},{16,20},{20,24},{24,28},{1,5},{5,9},{9,... | collective-permute-start | bytes 49160 | tf_op jit(solution)/shard_map/ppermute | solution.py:21
  245.9 6.0 %collective-permute-start.52 = (f32[2,1,16,128]{3,2,1,0:T(8,128)S(1)}, f32[2,1,16,128]{3,2,1,0:T(8,128)S(1)}, u32[]{:S(2)}, u32[]{:S(2)}) collective-permute-start(f32[2,1,16,128]{3,2,1,0:T(8,128)S(1)} %get-tuple-element.179), channel_id=1, source_target_pairs={{0,4},{4,8},{8,12},{12,16},{16,20},{20,24},{24,28},{1,5},{5,9},{9,... | collective-permute-start | bytes 49160 | tf_op jit(solution)/shard_map/ppermute | solution.py:21
  263.0 6.0 %collective-permute-start.56 = (f32[2,1,16,128]{3,2,1,0:T(8,128)S(1)}, f32[2,1,16,128]{3,2,1,0:T(8,128)S(1)}, u32[]{:S(2)}, u32[]{:S(2)}) collective-permute-start(f32[2,1,16,128]{3,2,1,0:T(8,128)S(1)} %get-tuple-element.175), channel_id=1, source_target_pairs={{0,4},{4,8},{8,12},{12,16},{16,20},{20,24},{24,28},{1,5},{5,9},{9,... | collective-permute-start | bytes 49160 | tf_op jit(solution)/shard_map/ppermute | solution.py:21
  280.1 6.0 %collective-permute-start.60 = (f32[2,1,16,128]{3,2,1,0:T(8,128)S(1)}, f32[2,1,16,128]{3,2,1,0:T(8,128)S(1)}, u32[]{:S(2)}, u32[]{:S(2)}) collective-permute-start(f32[2,1,16,128]{3,2,1,0:T(8,128)S(1)} %get-tuple-element.171), channel_id=1, source_target_pairs={{0,4},{4,8},{8,12},{12,16},{16,20},{20,24},{24,28},{1,5},{5,9},{9,... | collective-permute-start | bytes 49160 | tf_op jit(solution)/shard_map/ppermute | solution.py:21
  297.2 6.0 %collective-permute-start.64 = (f32[2,1,16,128]{3,2,1,0:T(8,128)S(1)}, f32[2,1,16,128]{3,2,1,0:T(8,128)S(1)}, u32[]{:S(2)}, u32[]{:S(2)}) collective-permute-start(f32[2,1,16,128]{3,2,1,0:T(8,128)S(1)} %get-tuple-element.167), channel_id=1, source_target_pairs={{0,4},{4,8},{8,12},{12,16},{16,20},{20,24},{24,28},{1,5},{5,9},{9,... | collective-permute-start | bytes 49160 | tf_op jit(solution)/shard_map/ppermute | solution.py:21
  314.3 6.0 %collective-permute-start.68 = (f32[2,1,16,128]{3,2,1,0:T(8,128)S(1)}, f32[2,1,16,128]{3,2,1,0:T(8,128)S(1)}, u32[]{:S(2)}, u32[]{:S(2)}) collective-permute-start(f32[2,1,16,128]{3,2,1,0:T(8,128)S(1)} %get-tuple-element.163), channel_id=1, source_target_pairs={{0,4},{4,8},{8,12},{12,16},{16,20},{20,24},{24,28},{1,5},{5,9},{9,... | collective-permute-start | bytes 49160 | tf_op jit(solution)/shard_map/ppermute | solution.py:21
  331.4 6.0 %collective-permute-start.72 = (f32[2,1,16,128]{3,2,1,0:T(8,128)S(1)}, f32[2,1,16,128]{3,2,1,0:T(8,128)S(1)}, u32[]{:S(2)}, u32[]{:S(2)}) collective-permute-start(f32[2,1,16,128]{3,2,1,0:T(8,128)S(1)} %get-tuple-element.159), channel_id=1, source_target_pairs={{0,4},{4,8},{8,12},{12,16},{16,20},{20,24},{24,28},{1,5},{5,9},{9,... | collective-permute-start | bytes 49160 | tf_op jit(solution)/shard_map/ppermute | solution.py:21
  347.4 6.0 %collective-permute-start.76 = (f32[2,1,16,128]{3,2,1,0:T(8,128)S(1)}, f32[2,1,16,128]{3,2,1,0:T(8,128)S(1)}, u32[]{:S(2)}, u32[]{:S(2)}) collective-permute-start(f32[2,1,16,128]{3,2,1,0:T(8,128)S(1)} %get-tuple-element.155), channel_id=1, source_target_pairs={{0,4},{4,8},{8,12},{12,16},{16,20},{20,24},{24,28},{1,5},{5,9},{9,... | collective-permute-start | bytes 49160 | tf_op jit(solution)/shard_map/ppermute | solution.py:21
  363.3 6.0 %collective-permute-start.80 = (f32[2,1,16,128]{3,2,1,0:T(8,128)S(1)}, f32[2,1,16,128]{3,2,1,0:T(8,128)S(1)}, u32[]{:S(2)}, u32[]{:S(2)}) collective-permute-start(f32[2,1,16,128]{3,2,1,0:T(8,128)S(1)} %get-tuple-element.151), channel_id=1, source_target_pairs={{0,4},{4,8},{8,12},{12,16},{16,20},{20,24},{24,28},{1,5},{5,9},{9,... | collective-permute-start | bytes 49160 | tf_op jit(solution)/shard_map/ppermute | solution.py:21
  380.6 6.6 %collective-permute-start.84 = (f32[2,1,16,128]{3,2,1,0:T(8,128)}, f32[2,1,16,128]{3,2,1,0:T(8,128)}, u32[]{:S(2)}, u32[]{:S(2)}) collective-permute-start(f32[2,1,16,128]{3,2,1,0:T(8,128)} %get-tuple-element.147), channel_id=1, source_target_pairs={{0,4},{4,8},{8,12},{12,16},{16,20},{20,24},{24,28},{1,5},{5,9},{9,... | collective-permute-start | bytes 49160 | tf_op jit(solution)/shard_map/ppermute | solution.py:21
  409.2 6.4 %collective-permute-start.88 = (f32[2,1,16,128]{3,2,1,0:T(8,128)}, f32[2,1,16,128]{3,2,1,0:T(8,128)}, u32[]{:S(2)}, u32[]{:S(2)}) collective-permute-start(f32[2,1,16,128]{3,2,1,0:T(8,128)} %get-tuple-element.143), channel_id=1, source_target_pairs={{0,4},{4,8},{8,12},{12,16},{16,20},{20,24},{24,28},{1,5},{5,9},{9,... | collective-permute-start | bytes 49160 | tf_op jit(solution)/shard_map/ppermute | solution.py:21
  417.5 8.8 %copy.36 = f32[2,32768]{0,1:T(8,128)} copy(f32[2,32768]{1,0:T(2,128)} %pad_maximum_fusion.307) | data formatting | bytes 524288 | tf_op jit(solution)/shard_map/stack | solution.py:53
  426.4 7.1 %gather_fusion.4 = f32[128,2]{1,0:T(8,128)} fusion(f32[2,32768]{0,1:T(8,128)} %copy.36, s32[1024]{0:T(1024)} %pad_clamp_fusion), kind=kCustom, calls=%fused_computation.4 | custom fusion | bytes 2560 | tf_op jit(solution)/shard_map/gather | solution.py:152
  446.0 5.5 collective-permute-start.92
  464.3 6.6 %collective-permute-start.96 = (f32[2,1,16,128]{3,2,1,0:T(8,128)}, f32[2,1,16,128]{3,2,1,0:T(8,128)}, u32[]{:S(2)}, u32[]{:S(2)}) collective-permute-start(f32[2,1,16,128]{3,2,1,0:T(8,128)} %get-tuple-element.135), channel_id=1, source_target_pairs={{0,4},{4,8},{8,12},{12,16},{16,20},{20,24},{24,28},{1,5},{5,9},{9,... | collective-permute-start | bytes 49160 | tf_op jit(solution)/shard_map/ppermute | solution.py:21
  472.9 8.8 %copy.35 = f32[2,32768]{0,1:T(8,128)} copy(f32[2,32768]{1,0:T(2,128)} %pad_maximum_fusion.306) | data formatting | bytes 524288 | tf_op jit(solution)/shard_map/stack | solution.py:53
  481.7 7.1 %gather_fusion.2 = f32[128,2]{1,0:T(8,128)} fusion(f32[2,32768]{0,1:T(8,128)} %copy.35, s32[1024]{0:T(1024)} %pad_clamp_fusion), kind=kCustom, calls=%fused_computation.2 | custom fusion | bytes 2560 | tf_op jit(solution)/shard_map/gather | solution.py:152
  509.6 4.8 collective-permute-start.102
  517.6 8.3 %copy.34 = f32[2,32768]{0,1:T(8,128)} copy(f32[2,32768]{1,0:T(2,128)S(1)} %pad_maximum_fusion.305) | data formatting | bytes 524288 | tf_op jit(solution)/shard_map/stack | solution.py:53
  525.9 6.5 %gather_fusion = f32[128,2]{1,0:T(8,128)S(1)} fusion(f32[2,32768]{0,1:T(8,128)} %copy.34, s32[1024]{0:T(1024)} %pad_clamp_fusion), kind=kCustom, calls=%fused_computation | custom fusion | bytes 2560 | tf_op jit(solution)/shard_map/gather | solution.py:152
  533.0 45.2 %all-reduce.51 = f32[64,3]{1,0:T(8,128)S(1)} all-reduce(f32[64,3]{1,0:T(8,128)S(1)} %fusion.588), channel_id=2, replica_groups=mesh['gx'=8,'gy'=4] {'gx','gy'}, use_global_device_ids=true, to_apply=%region_1.2.clone | all-reduce | flops 192 | bytes 1536
  (429 shorter events, 314.6 us)
Async XLA Ops:
  1.2 75.7 %collective-permute-start.7 = (f32[2,1,16,128]{3,2,1,0:T(8,128)}, f32[2,1,16,128]{3,2,1,0:T(8,128)S(1)}, u32[]{:S(2)}, u32[]{:S(2)}) collective-permute-start(f32[2,1,16,128]{3,2,1,0:T(8,128)} %broadcast.164), channel_id=1, source_target_pairs={{4,0},{8,4},{12,8},{16,12},{20,16},{24,20},{28,24},{5,1},{9,5},{13... | collective-permute-start | bytes 49160 | tf_op jit(solution)/shard_map/ppermute | solution.py:24
  2.5 74.4 %collective-permute-start.8 = (f32[2,1,16,128]{3,2,1,0:T(8,128)}, f32[2,1,16,128]{3,2,1,0:T(8,128)}, u32[]{:S(2)}, u32[]{:S(2)}) collective-permute-start(f32[2,1,16,128]{3,2,1,0:T(8,128)} %broadcast.164), channel_id=1, source_target_pairs={{0,4},{4,8},{8,12},{12,16},{16,20},{20,24},{24,28},{1,5},{5,9},{9,... | collective-permute-start | bytes 49160 | tf_op jit(solution)/shard_map/ppermute | solution.py:21
  8.5 12.2 %collective-permute-start.2 = (f32[2,3]{0,1:T(4,128)S(1)}, f32[2,3]{0,1:T(4,128)S(1)}, u32[]{:S(2)}, u32[]{:S(2)}) collective-permute-start(f32[2,3]{0,1:T(4,128)S(1)} %compare_select_fusion.1), channel_id=1, source_target_pairs={{0,31},{1,0},{2,1},{3,2},{4,3},{5,4},{6,5},{7,6},{8,7},{9,8},{10,9... | collective-permute-start | bytes 80 | tf_op jit(solution)/shard_map/ppermute | solution.py:104
  14.5 60.9 %collective-permute-start = (f32[1,16,128]{2,1,0:T(8,128)S(1)}, f32[1,16,128]{2,1,0:T(8,128)S(1)}, u32[]{:S(2)}, u32[]{:S(2)}) collective-permute-start(f32[1,16,128]{2,1,0:T(8,128)S(1)} %slice.1103), channel_id=1, source_target_pairs={{4,0},{8,4},{12,8},{16,12},{20,16},{24,20},{28,24},{5,1},{9,5},{13... | collective-permute-start | bytes 24584 | tf_op jit(solution)/shard_map/ppermute | solution.py:13
  16.6 58.8 %collective-permute-start.1 = (f32[16,1,128]{2,1,0:T(1,128)S(1)}, f32[16,1,128]{2,1,0:T(1,128)S(1)}, u32[]{:S(2)}, u32[]{:S(2)}) collective-permute-start(f32[16,1,128]{2,1,0:T(1,128)S(1)} %slice.1105), channel_id=1, source_target_pairs={{1,0},{2,1},{3,2},{5,4},{6,5},{7,6},{9,8},{10,9},{11,10},{13,12},{... | collective-permute-start | bytes 24584 | tf_op jit(solution)/shard_map/ppermute | solution.py:13
  211.8 7.2 %collective-permute-start.43 = (f32[2,1,16,128]{3,2,1,0:T(8,128)S(1)}, f32[2,1,16,128]{3,2,1,0:T(8,128)S(1)}, u32[]{:S(2)}, u32[]{:S(2)}) collective-permute-start(f32[2,1,16,128]{3,2,1,0:T(8,128)S(1)} %get-tuple-element.188), channel_id=1, source_target_pairs={{4,0},{8,4},{12,8},{16,12},{20,16},{24,20},{28,24},{5,1},{9,5},{13... | collective-permute-start | bytes 49160 | tf_op jit(solution)/shard_map/ppermute | solution.py:24
  227.5 7.4 %collective-permute-start.47 = (f32[2,1,16,128]{3,2,1,0:T(8,128)S(1)}, f32[2,1,16,128]{3,2,1,0:T(8,128)S(1)}, u32[]{:S(2)}, u32[]{:S(2)}) collective-permute-start(f32[2,1,16,128]{3,2,1,0:T(8,128)S(1)} %get-tuple-element.184), channel_id=1, source_target_pairs={{4,0},{8,4},{12,8},{16,12},{20,16},{24,20},{28,24},{5,1},{9,5},{13... | collective-permute-start | bytes 49160 | tf_op jit(solution)/shard_map/ppermute | solution.py:24
  228.8 6.9 %collective-permute-start.48 = (f32[2,1,16,128]{3,2,1,0:T(8,128)S(1)}, f32[2,1,16,128]{3,2,1,0:T(8,128)S(1)}, u32[]{:S(2)}, u32[]{:S(2)}) collective-permute-start(f32[2,1,16,128]{3,2,1,0:T(8,128)S(1)} %get-tuple-element.183), channel_id=1, source_target_pairs={{0,4},{4,8},{8,12},{12,16},{16,20},{20,24},{24,28},{1,5},{5,9},{9,... | collective-permute-start | bytes 49160 | tf_op jit(solution)/shard_map/ppermute | solution.py:21
  244.6 7.4 %collective-permute-start.51 = (f32[2,1,16,128]{3,2,1,0:T(8,128)S(1)}, f32[2,1,16,128]{3,2,1,0:T(8,128)S(1)}, u32[]{:S(2)}, u32[]{:S(2)}) collective-permute-start(f32[2,1,16,128]{3,2,1,0:T(8,128)S(1)} %get-tuple-element.180), channel_id=1, source_target_pairs={{4,0},{8,4},{12,8},{16,12},{20,16},{24,20},{28,24},{5,1},{9,5},{13... | collective-permute-start | bytes 49160 | tf_op jit(solution)/shard_map/ppermute | solution.py:24
  245.9 6.9 %collective-permute-start.52 = (f32[2,1,16,128]{3,2,1,0:T(8,128)S(1)}, f32[2,1,16,128]{3,2,1,0:T(8,128)S(1)}, u32[]{:S(2)}, u32[]{:S(2)}) collective-permute-start(f32[2,1,16,128]{3,2,1,0:T(8,128)S(1)} %get-tuple-element.179), channel_id=1, source_target_pairs={{0,4},{4,8},{8,12},{12,16},{16,20},{20,24},{24,28},{1,5},{5,9},{9,... | collective-permute-start | bytes 49160 | tf_op jit(solution)/shard_map/ppermute | solution.py:21
  261.7 7.4 %collective-permute-start.55 = (f32[2,1,16,128]{3,2,1,0:T(8,128)S(1)}, f32[2,1,16,128]{3,2,1,0:T(8,128)S(1)}, u32[]{:S(2)}, u32[]{:S(2)}) collective-permute-start(f32[2,1,16,128]{3,2,1,0:T(8,128)S(1)} %get-tuple-element.176), channel_id=1, source_target_pairs={{4,0},{8,4},{12,8},{16,12},{20,16},{24,20},{28,24},{5,1},{9,5},{13... | collective-permute-start | bytes 49160 | tf_op jit(solution)/shard_map/ppermute | solution.py:24
  263.0 6.9 %collective-permute-start.56 = (f32[2,1,16,128]{3,2,1,0:T(8,128)S(1)}, f32[2,1,16,128]{3,2,1,0:T(8,128)S(1)}, u32[]{:S(2)}, u32[]{:S(2)}) collective-permute-start(f32[2,1,16,128]{3,2,1,0:T(8,128)S(1)} %get-tuple-element.175), channel_id=1, source_target_pairs={{0,4},{4,8},{8,12},{12,16},{16,20},{20,24},{24,28},{1,5},{5,9},{9,... | collective-permute-start | bytes 49160 | tf_op jit(solution)/shard_map/ppermute | solution.py:21
  278.8 7.4 %collective-permute-start.59 = (f32[2,1,16,128]{3,2,1,0:T(8,128)S(1)}, f32[2,1,16,128]{3,2,1,0:T(8,128)S(1)}, u32[]{:S(2)}, u32[]{:S(2)}) collective-permute-start(f32[2,1,16,128]{3,2,1,0:T(8,128)S(1)} %get-tuple-element.172), channel_id=1, source_target_pairs={{4,0},{8,4},{12,8},{16,12},{20,16},{24,20},{28,24},{5,1},{9,5},{13... | collective-permute-start | bytes 49160 | tf_op jit(solution)/shard_map/ppermute | solution.py:24
  280.1 6.9 %collective-permute-start.60 = (f32[2,1,16,128]{3,2,1,0:T(8,128)S(1)}, f32[2,1,16,128]{3,2,1,0:T(8,128)S(1)}, u32[]{:S(2)}, u32[]{:S(2)}) collective-permute-start(f32[2,1,16,128]{3,2,1,0:T(8,128)S(1)} %get-tuple-element.171), channel_id=1, source_target_pairs={{0,4},{4,8},{8,12},{12,16},{16,20},{20,24},{24,28},{1,5},{5,9},{9,... | collective-permute-start | bytes 49160 | tf_op jit(solution)/shard_map/ppermute | solution.py:21
  295.9 7.4 %collective-permute-start.63 = (f32[2,1,16,128]{3,2,1,0:T(8,128)S(1)}, f32[2,1,16,128]{3,2,1,0:T(8,128)S(1)}, u32[]{:S(2)}, u32[]{:S(2)}) collective-permute-start(f32[2,1,16,128]{3,2,1,0:T(8,128)S(1)} %get-tuple-element.168), channel_id=1, source_target_pairs={{4,0},{8,4},{12,8},{16,12},{20,16},{24,20},{28,24},{5,1},{9,5},{13... | collective-permute-start | bytes 49160 | tf_op jit(solution)/shard_map/ppermute | solution.py:24
  297.2 6.9 %collective-permute-start.64 = (f32[2,1,16,128]{3,2,1,0:T(8,128)S(1)}, f32[2,1,16,128]{3,2,1,0:T(8,128)S(1)}, u32[]{:S(2)}, u32[]{:S(2)}) collective-permute-start(f32[2,1,16,128]{3,2,1,0:T(8,128)S(1)} %get-tuple-element.167), channel_id=1, source_target_pairs={{0,4},{4,8},{8,12},{12,16},{16,20},{20,24},{24,28},{1,5},{5,9},{9,... | collective-permute-start | bytes 49160 | tf_op jit(solution)/shard_map/ppermute | solution.py:21
  313.0 7.4 %collective-permute-start.67 = (f32[2,1,16,128]{3,2,1,0:T(8,128)S(1)}, f32[2,1,16,128]{3,2,1,0:T(8,128)S(1)}, u32[]{:S(2)}, u32[]{:S(2)}) collective-permute-start(f32[2,1,16,128]{3,2,1,0:T(8,128)S(1)} %get-tuple-element.164), channel_id=1, source_target_pairs={{4,0},{8,4},{12,8},{16,12},{20,16},{24,20},{28,24},{5,1},{9,5},{13... | collective-permute-start | bytes 49160 | tf_op jit(solution)/shard_map/ppermute | solution.py:24
  314.3 6.9 %collective-permute-start.68 = (f32[2,1,16,128]{3,2,1,0:T(8,128)S(1)}, f32[2,1,16,128]{3,2,1,0:T(8,128)S(1)}, u32[]{:S(2)}, u32[]{:S(2)}) collective-permute-start(f32[2,1,16,128]{3,2,1,0:T(8,128)S(1)} %get-tuple-element.163), channel_id=1, source_target_pairs={{0,4},{4,8},{8,12},{12,16},{16,20},{20,24},{24,28},{1,5},{5,9},{9,... | collective-permute-start | bytes 49160 | tf_op jit(solution)/shard_map/ppermute | solution.py:21
  330.1 7.4 %collective-permute-start.71 = (f32[2,1,16,128]{3,2,1,0:T(8,128)S(1)}, f32[2,1,16,128]{3,2,1,0:T(8,128)S(1)}, u32[]{:S(2)}, u32[]{:S(2)}) collective-permute-start(f32[2,1,16,128]{3,2,1,0:T(8,128)S(1)} %get-tuple-element.160), channel_id=1, source_target_pairs={{4,0},{8,4},{12,8},{16,12},{20,16},{24,20},{28,24},{5,1},{9,5},{13... | collective-permute-start | bytes 49160 | tf_op jit(solution)/shard_map/ppermute | solution.py:24
  346.1 7.4 %collective-permute-start.75 = (f32[2,1,16,128]{3,2,1,0:T(8,128)S(1)}, f32[2,1,16,128]{3,2,1,0:T(8,128)S(1)}, u32[]{:S(2)}, u32[]{:S(2)}) collective-permute-start(f32[2,1,16,128]{3,2,1,0:T(8,128)S(1)} %get-tuple-element.156), channel_id=1, source_target_pairs={{4,0},{8,4},{12,8},{16,12},{20,16},{24,20},{28,24},{5,1},{9,5},{13... | collective-permute-start | bytes 49160 | tf_op jit(solution)/shard_map/ppermute | solution.py:24
  362.0 8.1 %collective-permute-start.79 = (f32[2,1,16,128]{3,2,1,0:T(8,128)S(1)}, f32[2,1,16,128]{3,2,1,0:T(8,128)S(1)}, u32[]{:S(2)}, u32[]{:S(2)}) collective-permute-start(f32[2,1,16,128]{3,2,1,0:T(8,128)S(1)} %get-tuple-element.152), channel_id=1, source_target_pairs={{4,0},{8,4},{12,8},{16,12},{20,16},{24,20},{28,24},{5,1},{9,5},{13... | collective-permute-start | bytes 49160 | tf_op jit(solution)/shard_map/ppermute | solution.py:24
  379.1 16.2 %collective-permute-start.83 = (f32[2,1,16,128]{3,2,1,0:T(8,128)}, f32[2,1,16,128]{3,2,1,0:T(8,128)S(1)}, u32[]{:S(2)}, u32[]{:S(2)}) collective-permute-start(f32[2,1,16,128]{3,2,1,0:T(8,128)} %get-tuple-element.148), channel_id=1, source_target_pairs={{4,0},{8,4},{12,8},{16,12},{20,16},{24,20},{28,24},{5,1},{9,5},{13... | collective-permute-start | bytes 49160 | tf_op jit(solution)/shard_map/ppermute | solution.py:24
  380.6 14.7 %collective-permute-start.84 = (f32[2,1,16,128]{3,2,1,0:T(8,128)}, f32[2,1,16,128]{3,2,1,0:T(8,128)}, u32[]{:S(2)}, u32[]{:S(2)}) collective-permute-start(f32[2,1,16,128]{3,2,1,0:T(8,128)} %get-tuple-element.147), channel_id=1, source_target_pairs={{0,4},{4,8},{8,12},{12,16},{16,20},{20,24},{24,28},{1,5},{5,9},{9,... | collective-permute-start | bytes 49160 | tf_op jit(solution)/shard_map/ppermute | solution.py:21
  396.3 7.1 %collective-permute-start.85 = (f32[2,18,1,128]{3,2,1,0:T(1,128)S(1)}, f32[2,18,1,128]{3,2,1,0:T(1,128)S(1)}, u32[]{:S(2)}, u32[]{:S(2)}) collective-permute-start(f32[2,18,1,128]{3,2,1,0:T(1,128)S(1)} %get-tuple-element.89), channel_id=1, source_target_pairs={{1,0},{2,1},{3,2},{5,4},{6,5},{7,6},{9,8},{10,9},{11,10},{13,12},{... | collective-permute-start | bytes 55304 | tf_op jit(solution)/shard_map/ppermute | solution.py:24
  407.9 25.6 %collective-permute-start.87 = (f32[2,1,16,128]{3,2,1,0:T(8,128)}, f32[2,1,16,128]{3,2,1,0:T(8,128)S(1)}, u32[]{:S(2)}, u32[]{:S(2)}) collective-permute-start(f32[2,1,16,128]{3,2,1,0:T(8,128)} %get-tuple-element.144), channel_id=1, source_target_pairs={{4,0},{8,4},{12,8},{16,12},{20,16},{24,20},{28,24},{5,1},{9,5},{13... | collective-permute-start | bytes 49160 | tf_op jit(solution)/shard_map/ppermute | solution.py:24
  409.2 24.3 %collective-permute-start.88 = (f32[2,1,16,128]{3,2,1,0:T(8,128)}, f32[2,1,16,128]{3,2,1,0:T(8,128)}, u32[]{:S(2)}, u32[]{:S(2)}) collective-permute-start(f32[2,1,16,128]{3,2,1,0:T(8,128)} %get-tuple-element.143), channel_id=1, source_target_pairs={{0,4},{4,8},{8,12},{12,16},{16,20},{20,24},{24,28},{1,5},{5,9},{9,... | collective-permute-start | bytes 49160 | tf_op jit(solution)/shard_map/ppermute | solution.py:21
  434.5 7.1 %collective-permute-start.89 = (f32[2,18,1,128]{3,2,1,0:T(1,128)S(1)}, f32[2,18,1,128]{3,2,1,0:T(1,128)S(1)}, u32[]{:S(2)}, u32[]{:S(2)}) collective-permute-start(f32[2,18,1,128]{3,2,1,0:T(1,128)S(1)} %get-tuple-element.87), channel_id=1, source_target_pairs={{1,0},{2,1},{3,2},{5,4},{6,5},{7,6},{9,8},{10,9},{11,10},{13,12},{... | collective-permute-start | bytes 55304 | tf_op jit(solution)/shard_map/ppermute | solution.py:24
  444.7 8.4 %collective-permute-start.91 = (f32[2,1,16,128]{3,2,1,0:T(8,128)S(1)}, f32[2,1,16,128]{3,2,1,0:T(8,128)S(1)}, u32[]{:S(2)}, u32[]{:S(2)}) collective-permute-start(f32[2,1,16,128]{3,2,1,0:T(8,128)S(1)} %get-tuple-element.140), channel_id=1, source_target_pairs={{4,0},{8,4},{12,8},{16,12},{20,16},{24,20},{28,24},{5,1},{9,5},{13... | collective-permute-start | bytes 49160 | tf_op jit(solution)/shard_map/ppermute | solution.py:24
  446.0 7.1 %collective-permute-start.92 = (f32[2,1,16,128]{3,2,1,0:T(8,128)S(1)}, f32[2,1,16,128]{3,2,1,0:T(8,128)S(1)}, u32[]{:S(2)}, u32[]{:S(2)}) collective-permute-start(f32[2,1,16,128]{3,2,1,0:T(8,128)S(1)} %get-tuple-element.139), channel_id=1, source_target_pairs={{0,4},{4,8},{8,12},{12,16},{16,20},{20,24},{24,28},{1,5},{5,9},{9,... | collective-permute-start | bytes 49160 | tf_op jit(solution)/shard_map/ppermute | solution.py:21
  463.0 25.8 %collective-permute-start.95 = (f32[2,1,16,128]{3,2,1,0:T(8,128)}, f32[2,1,16,128]{3,2,1,0:T(8,128)S(1)}, u32[]{:S(2)}, u32[]{:S(2)}) collective-permute-start(f32[2,1,16,128]{3,2,1,0:T(8,128)} %get-tuple-element.136), channel_id=1, source_target_pairs={{4,0},{8,4},{12,8},{16,12},{20,16},{24,20},{28,24},{5,1},{9,5},{13... | collective-permute-start | bytes 49160 | tf_op jit(solution)/shard_map/ppermute | solution.py:24
  464.3 24.5 %collective-permute-start.96 = (f32[2,1,16,128]{3,2,1,0:T(8,128)}, f32[2,1,16,128]{3,2,1,0:T(8,128)}, u32[]{:S(2)}, u32[]{:S(2)}) collective-permute-start(f32[2,1,16,128]{3,2,1,0:T(8,128)} %get-tuple-element.135), channel_id=1, source_target_pairs={{0,4},{4,8},{8,12},{12,16},{16,20},{20,24},{24,28},{1,5},{5,9},{9,... | collective-permute-start | bytes 49160 | tf_op jit(solution)/shard_map/ppermute | solution.py:21
  489.8 7.1 %collective-permute-start.97 = (f32[2,18,1,128]{3,2,1,0:T(1,128)S(1)}, f32[2,18,1,128]{3,2,1,0:T(1,128)S(1)}, u32[]{:S(2)}, u32[]{:S(2)}) collective-permute-start(f32[2,18,1,128]{3,2,1,0:T(1,128)S(1)} %get-tuple-element.83), channel_id=1, source_target_pairs={{1,0},{2,1},{3,2},{5,4},{6,5},{7,6},{9,8},{10,9},{11,10},{13,12},{... | collective-permute-start | bytes 55304 | tf_op jit(solution)/shard_map/ppermute | solution.py:24
  (115 other events, 1954.2 us)
